TPU v7x, 32 devices: a whole 2x2x4 slice. The times are simulated.
32 devices in a mesh: replica: 16 (over z, y, core), tp: 2 (over x).
Axes of the slice: x: 2, y: 2, z: 4, core: 2. Of those that a mesh axis runs over, the one named last changes fastest.
Arguments:
- states: bfloat16 [8, 256, 4608], P(None, 'replica'), may hold values from -6 to 6
- pre_gain: float32 [4608], replicated, may hold values from 0.5 to 1.5
- post_gain: float32 [4608], replicated, may hold values from 0.5 to 1.5
- query_weight: bfloat16 [4608, 2048], P(None, 'tp'), may hold values from -0.09375 to 0.09375
- key_weight: bfloat16 [4608, 1024], P(None, 'tp'), may hold values from -0.09375 to 0.09375
- value_weight: bfloat16 [4608, 1024], P(None, 'tp'), may hold values from -0.09375 to 0.09375
- out_weight: bfloat16 [2048, 4608], P('tp')
- cache_keys: bfloat16 [4096, 16, 1024], P('replica', None, 'tp'), may hold values from -6 to 6
- cache_values: bfloat16 [4096, 16, 1024], P('replica', None, 'tp'), may hold values from -6 to 6
- context: int32 [256], replicated, may hold values from 1 to 248
- slot_map: int32 [8, 256], replicated, may hold values from 0 to 255, each once within a row
Outputs:
- decoded: bfloat16 [8, 256, 4608], P(None, 'replica')
- moved_keys: bfloat16 [4096, 16, 1024], P('replica', None, 'tp')
- moved_values: bfloat16 [4096, 16, 1024], P('replica', None, 'tp')
Inputs may be any that keep to these rules, and one draw needn't show every extreme that they name: `slot_map`: each row names every page of one replica set once.
All inputs are finite; a program needn't handle non-finite values.
Results may differ from a plain program's by a relative error of at most 0.012.
Values may be sent and summed in bfloat16 or wider, within the bound.
A program may use at most 128 MiB of HBM per device.

v0:
```python
import functools
import math

import jax
import jax.numpy as jnp
from jax import lax
from jax.experimental import pallas as pl
from jax.experimental.pallas import tpu as pltpu
from jax.sharding import PartitionSpec as P

HD = 128


epsilon = 1e-06
softcap = 50.0
query_scalar = 144.0


def shifted(value, axis, steps):
    count = lax.axis_size(axis)
    initial, last = (max(0, -steps), min(count, count - steps))
    return lax.ppermute(value, axis, [(source, source + steps) for source in range(initial, last)])


def rotate(vectors, positions):
    halfway = vectors.shape[-1] // 2
    frequency = 10000.0 ** (-jnp.arange(halfway, dtype=jnp.float32) / halfway)
    angles = (positions.astype(jnp.float32)[:, None] * frequency[None, :])[:, None, :]
    cosine = jnp.cos(angles)
    sines = jnp.sin(angles)
    leading = vectors[..., :halfway]
    trailing = vectors[..., halfway:]
    return jnp.concatenate(
        [leading * cosine - trailing * sines, trailing * cosine + leading * sines], axis=-1
    )


def write_rows(cache, rows, lengths):
    grid = jnp.arange(cache.shape[1], dtype=jnp.int32)[None, :] - lengths[:, None]
    for step in range(rows.shape[1]):
        cache = jnp.where((grid == step)[:, :, None], rows[:, step][:, None, :], cache)
    return cache


def place_kernel(pages, group, slots, flag, own, received, *rest):
    out, held, in_sem, out_sem = rest[-4:]
    groups = [(low, min(group, pages - low)) for low in range(0, pages, group)]

    def load(source):
        for index, (low, count) in enumerate(groups):
            pltpu.make_async_copy(
                source.at[pl.ds(low, count)], held.at[pl.ds(low, count)], in_sem.at[index]
            ).start()

    @pl.when(flag[0] != 0)
    def _():
        load(received)

    @pl.when(flag[0] == 0)
    def _():
        load(own)

    for index, (low, count) in enumerate(groups):
        pltpu.make_async_copy(
            own.at[pl.ds(low, count)], held.at[pl.ds(low, count)], in_sem.at[index]
        ).wait()

        def send(page, carry):
            pltpu.make_async_copy(held.at[page], out.at[slots[page]], out_sem).start()
            return carry

        lax.fori_loop(low, low + count, send, 0, unroll=8)
    pltpu.make_async_copy(held, held, out_sem).wait()


def place(region, slots, flag, own, received, total):
    pages = own.shape[0]
    group = 16
    anywhere = pl.BlockSpec(memory_space=pltpu.MemorySpace.HBM)
    scalar = pl.BlockSpec(memory_space=pltpu.SMEM)
    operands = (slots, flag, own, received) + (() if region is None else (region,))
    return pl.pallas_call(
        functools.partial(place_kernel, pages, group),
        out_shape=jax.ShapeDtypeStruct((total,) + own.shape[1:], own.dtype),
        in_specs=[scalar, scalar] + [anywhere] * (len(operands) - 2),
        out_specs=anywhere,
        scratch_shapes=[
            pltpu.VMEM(own.shape, own.dtype),
            pltpu.SemaphoreType.DMA((-(-pages // group),)),
            pltpu.SemaphoreType.DMA,
        ],
        input_output_aliases={} if region is None else {4: 0},
        cost_estimate=pl.CostEstimate(
            flops=0, bytes_accessed=2 * own.size * 2, transcendentals=0
        ),
    )(*operands)


def shards(
    states,
    pre_gain,
    post_gain,
    query_weight,
    key_weight,
    value_weight,
    out_weight,
    cache_keys,
    cache_values,
    context,
    slot_map,
):
    half_count = lax.axis_size("replica") // 2
    tp_count = lax.axis_size("tp")
    replica = lax.axis_index("replica")
    partner = replica % half_count
    steps, requests, model_width = states.shape
    page_count, page_len, kv_width = cache_keys.shape
    per_request = page_count // requests
    length = per_request * page_len
    kv_local = kv_width // HD
    q_local = query_weight.shape[1] // HD
    group_size = q_local // kv_local
    own_lengths = lax.dynamic_slice_in_dim(context, replica * requests, requests)
    pair_lengths = lax.dynamic_slice_in_dim(context, partner * requests, requests)
    slot_ids = lax.dynamic_index_in_dim(slot_map, partner, 0, keepdims=False)
    is_target = replica >= half_count
    slots = jnp.where(is_target, slot_ids, jnp.arange(page_count, dtype=jnp.int32))
    flag = is_target.astype(jnp.int32).reshape(1)

    def paged(rows):
        return rows.reshape(-1, page_len, kv_width)

    def shift(value):
        return shifted(value, "replica", half_count)

    early = max(1, requests // 8)
    late = max(1, requests // 16)
    cuts = ((0, early), (early, requests - late), (requests - late, requests))
    caches = {
        "v": cache_values.reshape(requests, length, kv_width),
        "k": cache_keys.reshape(requests, length, kv_width),
    }
    early_rows = {name: paged(caches[name][:early]) for name in caches}
    states, caches, early_rows = lax.optimization_barrier((states, caches, early_rows))
    raw = {name: shift(early_rows[name]) for name in caches}

    rows_first = states.transpose(1, 0, 2)
    widened = rows_first.astype(jnp.float32)
    squares = jnp.mean(widened * widened, axis=-1, keepdims=True)
    normed = (
        widened
        * lax.rsqrt(squares + epsilon)
        * pre_gain
    ).astype(jnp.bfloat16).reshape(requests * steps, model_width)
    positions = own_lengths[:, None] + jnp.arange(steps, dtype=jnp.int32)[None, :]
    flat_positions = positions.reshape(-1)

    new = {}
    new["v"] = (
        jnp.dot(normed, value_weight, preferred_element_type=jnp.float32)
        .astype(jnp.bfloat16)
        .reshape(requests, steps, kv_width)
    )
    keys = jnp.dot(normed, key_weight, preferred_element_type=jnp.float32)
    new["k"] = (
        rotate(keys.reshape(-1, kv_local, HD), flat_positions)
        .astype(jnp.bfloat16)
        .reshape(requests, steps, kv_width)
    )
    own = {
        name: [
            write_rows(caches[name][low:high], new[name][low:high], own_lengths[low:high])
            for low, high in cuts
        ]
        for name in caches
    }
    middle = {name: shift(paged(own[name][1])) for name in caches}
    delta = shift(jnp.stack([new["k"][:early], new["v"][:early]]))

    queries = jnp.dot(normed, query_weight, preferred_element_type=jnp.float32)
    queries = (
        rotate(queries.reshape(-1, q_local, HD), flat_positions)
        .astype(jnp.bfloat16)
        .reshape(requests, steps, kv_local, group_size, HD)
    )
    grid = jnp.arange(length, dtype=jnp.int32)
    visible = grid[None, None, :] <= positions[:, :, None]
    outs = []
    for index, (low, high) in enumerate(cuts):
        key_view = own["k"][index].reshape(high - low, length, kv_local, HD)
        value_view = own["v"][index].reshape(high - low, length, kv_local, HD)
        scores = jnp.einsum(
            "rtkgd,rlkd->rktgl", queries[low:high], key_view, preferred_element_type=jnp.float32
        )
        scores = softcap * jnp.tanh(scores / (softcap * math.sqrt(query_scalar)))
        expo = jnp.where(visible[low:high, None, :, None, :], jnp.exp(scores), 0.0)
        weights = (expo / jnp.sum(expo, axis=-1, keepdims=True)).astype(jnp.bfloat16)
        attended = jnp.einsum(
            "rktgl,rlkd->rtkgd", weights, value_view, preferred_element_type=jnp.float32
        )
        outs.append(attended.astype(jnp.bfloat16).reshape((high - low) * steps, q_local * HD))
    attended = jnp.concatenate(outs, axis=0)
    partial_sum = jnp.dot(attended, out_weight, preferred_element_type=jnp.float32).astype(
        jnp.bfloat16
    )
    summed = partial_sum.astype(jnp.float32)
    for offset in range(1, tp_count):
        ring = [(source, (source + offset) % tp_count) for source in range(tp_count)]
        summed = summed + lax.ppermute(partial_sum, "tp", ring).astype(jnp.float32)
    inverse = lax.rsqrt(jnp.mean(summed * summed, axis=-1, keepdims=True) + epsilon)
    moved = (summed * inverse * post_gain).reshape(requests, steps, model_width)
    decoded = (widened + moved).astype(jnp.bfloat16).transpose(1, 0, 2)

    last_k, last_v, decoded = lax.optimization_barrier((own["k"][2], own["v"][2], decoded))
    last = {"v": shift(paged(last_v)), "k": shift(paged(last_k))}

    results = {}
    for name, part in (("v", 1), ("k", 0)):
        first = write_rows(
            raw[name].reshape(early, length, kv_width), delta[part], pair_lengths[:early]
        )
        region = None
        received = (paged(first), middle[name], last[name])
        for index, (low, high) in enumerate(cuts):
            region = place(
                region,
                slots[low * per_request : high * per_request],
                flag,
                paged(own[name][index]),
                received[index],
                page_count,
            )
        results[name] = region
    return (decoded, results["k"], results["v"])


def solution(mesh):
    return jax.shard_map(
        shards,
        mesh=mesh,
        in_specs=(
            P(None, "replica", None),
            P(),
            P(),
            P(None, "tp"),
            P(None, "tp"),
            P(None, "tp"),
            P("tp", None),
            P("replica", None, "tp"),
            P("replica", None, "tp"),
            P(),
            P(),
        ),
        out_specs=(P(None, "replica", None), P("replica", None, "tp"), P("replica", None, "tp")),
        check_vma=False,
    )
```

profile of v0, /device:TPU:27, one launch (start us, length us, event | category | flops | bytes accessed | tf_op | source)
XLA Modules:
  0.0 397.3 jit_solution(10230554252949686750)
XLA Ops:
  0.7 1.9 slice.328
  2.5 1.9 slice.329
  4.4 2.6 fusion.1
  7.0 1.3 fusion.89
  8.6 3.9 fusion.15
  13.2 4.7 %select_select_fusion.1 = bf16[13,256,512]{2,1,0:T(8,128)(2,1)S(1)} fusion(bf16[16,256,512]{2,1,0:T(8,128)(2,1)S(1)} %bitcast.289, pred[13,256]{1,0:T(8,128)(4,1)S(1)} %get-tuple-element.118, pred[13,256]{1,0:T(8,128)(4,1)S(1)} %get-tuple-element.119, pred[13,256]{1,0:T(8,128)(4,1)S(1)} %get-tuple-element.120, pred[13,256]{1,0:T(8,128)(4,1)S(1)} %get-tuple-element.121, ...), kind=kLoop, calls=%fused_computation.2 | loop fusion | flops 13631488 | bytes 6948864 | tf_op jit(solution)/shard_map/jit(_where)/select_n | solution.py:41
  20.0 6.7 %copy.162 = bf16[512,4608]{1,0:T(8,128)(2,1)} copy(bf16[512,4608]{0,1:T(8,128)(2,1)} %bitcast.290) | data formatting | bytes 9437184 | tf_op jit(solution)/shard_map/dot_general | solution.py:164
  26.8 4.2 %fusion.11 = f32[128,4,128]{0,2,1:T(8,128)S(1)} fusion(bf16[4,128,4608]{2,1,0:T(8,128)(2,1)} %bitcast.291, f32[4608]{0:T(1024)S(1)} %copy-done.29, f32[16,8]{1,0:T(8,128)S(1)} %add_rsqrt_fusion, bf16[8,16,4608]{2,1,0:T(8,128)(2,1)} %param.11), kind=kOutput, calls=%fused_computation.21 | convolution fusion | flops 606339072 | bytes 6179328 | tf_op jit(solution)/shard_map/dot_general | solution.py:164
  32.6 1.7 copy.143
  34.3 1.6 slice.398
  35.8 1.7 fusion.83
  37.6 6.9 %select_select_fusion = bf16[13,256,512]{2,1,0:T(8,128)(2,1)} fusion(bf16[16,256,512]{2,1,0:T(8,128)(2,1)} %bitcast.284, pred[13,256]{1,0:T(8,128)(4,1)S(1)} %get-tuple-element.118, pred[13,256]{1,0:T(8,128)(4,1)} %copy-done.14, pred[13,256]{1,0:T(8,128)(4,1)} %copy-done.15, pred[13,256]{1,0:T(8,128)(4,1)} %copy-done.16, pred[13,256]{1,0:T(8,128)(4,1)} %copy-done.17, ...), kind=kLoop, calls=%fused_computation.1 | loop fusion | flops 13631488 | bytes 6948864 | tf_op jit(solution)/shard_map/jit(_where)/select_n | solution.py:41
  44.6 1.5 collective-permute-start.2
  48.1 5.5 %copy.144 = bf16[13,256,512]{1,2,0:T(8,128)(2,1)} copy(bf16[13,256,512]{2,1,0:T(8,128)(2,1)} %select_select_fusion) | data formatting | bytes 6815744 | tf_op jit(solution)/shard_map/jit(_where)/select_n | solution.py:41
  53.6 12.5 %copy.165 = bf16[1024,4608]{1,0:T(8,128)(2,1)} copy(bf16[1024,4608]{0,1:T(8,128)(2,1)} %bitcast.282) | data formatting | bytes 18874368 | tf_op jit(solution)/shard_map/dot_general | solution.py:180
  66.1 5.7 %fusion.9 = f32[128,8,128]{0,2,1:T(8,128)S(1)} fusion(bf16[8,128,4608]{2,1,0:T(8,128)(2,1)} %bitcast.283, f32[4608]{0:T(1024)S(1)} %copy-done.30, f32[16,8]{1,0:T(8,128)S(1)} %copy-done.24, bf16[8,16,4608]{2,1,0:T(8,128)(2,1)} %param.11), kind=kOutput, calls=%fused_computation.19 | convolution fusion | flops 1210318848 | bytes 11160064 | tf_op jit(solution)/shard_map/dot_general | solution.py:180
  74.2 3.5 copy.141
  77.7 1.7 pad_maximum_fusion
  88.7 1.6 copy.128
  91.0 1.6 fusion.88
  95.1 2.4 select_select_fusion.4
  97.5 2.0 copy.129
  99.5 1.7 copy.127
  104.0 2.4 select_select_fusion.5
  106.3 2.0 copy.125
  108.4 1.8 copy.142
  110.9 2.0 select_select_fusion.7
  112.9 1.8 copy.149
  115.7 2.0 select_select_fusion.6
  117.7 1.8 copy.148
  119.5 1.9 fusion.21
  121.4 1.4 convolution_convert_fusion.2
  122.9 3.6 fusion.7
  126.4 4.2 %convolution_convert_fusion.1 = bf16[13,4,128,8,2]{2,3,4,1,0:T(8,128)(2,1)} fusion(bf16[13,256,4,128,1]{1,3,4,2,0:T(8,128)(2,1)} %bitcast.294, f32[13,4,8,2,256]{4,2,3,1,0:T(8,128)} %fusion.7), kind=kOutput, calls=%fused_computation.17 | convolution fusion | flops 55059520 | bytes 4472832 | tf_op jit(solution)/shard_map/rktgl,rlkd->rtkgd/dot_general | solution.py:198
  133.1 6.3 %convolution_convert_fusion = bf16[128,4608]{1,0:T(8,128)(2,1)} fusion(bf16[1024,4608]{1,0:T(8,128)(2,1)} %param.17, bf16[8,1024]{1,0:T(8,128)(2,1)S(1)} %bitcast.320, bf16[104,1024]{1,0:T(8,128)(2,1)} %bitcast.301, bf16[16,1024]{1,0:T(8,128)(2,1)S(1)} %bitcast.319), kind=kOutput, calls=%fused_computation | convolution fusion | flops 1209335808 | bytes 10878976 | tf_op jit(solution)/shard_map/dot_general | solution.py:203
  144.4 206.1 %collective-permute-done.3 = bf16[2,2,8,512]{3,2,1,0:T(8,128)(2,1)S(1)} collective-permute-done((bf16[2,2,8,512]{3,2,1,0:T(8,128)(2,1)S(1)}, bf16[2,2,8,512]{3,2,1,0:T(8,128)(2,1)S(1)}, u32[]{:S(2)}, u32[]{:S(2)}) %collective-permute-start.3) | collective-permute-done | bytes 32800 | tf_op jit(solution)/shard_map/ppermute | solution.py:22
  352.0 9.8 %collective-permute-done.7 = bf16[32,16,512]{2,1,0:T(8,128)(2,1)} collective-permute-done((bf16[32,16,512]{2,1,0:T(8,128)(2,1)}, bf16[32,16,512]{2,1,0:T(8,128)(2,1)}, u32[]{:S(2)}, u32[]{:S(2)}) %collective-permute-start.7) | collective-permute-done | bytes 524320 | tf_op jit(solution)/shard_map/ppermute | solution.py:22
  361.9 3.6 select_select_fusion.2.received
  365.5 2.5 shard_map.133.rest_0_
  368.0 2.1 multiply_reduce_fusion
  370.1 3.9 fusion.8
  376.7 3.6 select_select_fusion.3.received
  380.3 2.4 shard_map.130.rest_0_
  382.7 2.6 copy.154
  385.3 3.5 shard_map.134.rest_0_
  388.9 3.5 shard_map.131.rest_0_
  392.4 2.3 shard_map.135
  394.8 2.3 shard_map.132
  (173 shorter events, 37.2 us)
Async XLA Ops:
  0.6 141.6 %copy-start = (s32[8,256]{1,0:T(8,128)S(1)}, s32[8,256]{1,0:T(8,128)}, u32[]{:S(2)}) copy-start(s32[8,256]{1,0:T(8,128)} %param.21) | copy-start | bytes 24580
  7.0 19.8 %copy-start.23 = (f32[16,8]{1,0:T(8,128)}, f32[16,8]{1,0:T(8,128)S(1)}, u32[]{:S(2)}) copy-start(f32[16,8]{1,0:T(8,128)S(1)} %add_rsqrt_fusion) | copy-start | bytes 1540
  8.3 10.9 %copy-start.25 = (s32[16]{0:T(128)}, s32[16]{0:T(128)S(1)}, u32[]{:S(2)}) copy-start(s32[16]{0:T(128)S(1)} %get-tuple-element.106) | copy-start | bytes 196
  8.5 4.7 %copy-start.14 = (pred[13,256]{1,0:T(8,128)(4,1)}, pred[13,256]{1,0:T(8,128)(4,1)S(1)}, u32[]{:S(2)}) copy-start(pred[13,256]{1,0:T(8,128)(4,1)S(1)} %get-tuple-element.119) | copy-start | bytes 9988
  8.5 4.7 %copy-start.15 = (pred[13,256]{1,0:T(8,128)(4,1)}, pred[13,256]{1,0:T(8,128)(4,1)S(1)}, u32[]{:S(2)}) copy-start(pred[13,256]{1,0:T(8,128)(4,1)S(1)} %get-tuple-element.120) | copy-start | bytes 9988
  8.5 4.7 %copy-start.16 = (pred[13,256]{1,0:T(8,128)(4,1)}, pred[13,256]{1,0:T(8,128)(4,1)S(1)}, u32[]{:S(2)}) copy-start(pred[13,256]{1,0:T(8,128)(4,1)S(1)} %get-tuple-element.121) | copy-start | bytes 9988
  8.5 4.7 %copy-start.17 = (pred[13,256]{1,0:T(8,128)(4,1)}, pred[13,256]{1,0:T(8,128)(4,1)S(1)}, u32[]{:S(2)}) copy-start(pred[13,256]{1,0:T(8,128)(4,1)S(1)} %get-tuple-element.122) | copy-start | bytes 9988
  8.5 4.6 %copy-start.18 = (pred[13,256]{1,0:T(8,128)(4,1)}, pred[13,256]{1,0:T(8,128)(4,1)S(1)}, u32[]{:S(2)}) copy-start(pred[13,256]{1,0:T(8,128)(4,1)S(1)} %get-tuple-element.123) | copy-start | bytes 9988
  8.5 4.6 %copy-start.19 = (pred[13,256]{1,0:T(8,128)(4,1)}, pred[13,256]{1,0:T(8,128)(4,1)S(1)}, u32[]{:S(2)}) copy-start(pred[13,256]{1,0:T(8,128)(4,1)S(1)} %get-tuple-element.124) | copy-start | bytes 9988
  8.6 4.6 %copy-start.2 = (bf16[256,16,512]{2,1,0:T(8,128)(2,1)S(1)}, bf16[256,16,512]{2,1,0:T(8,128)(2,1)}, u32[]{:S(2)}) copy-start(bf16[256,16,512]{2,1,0:T(8,128)(2,1)} %param.19) | copy-start | bytes 12582916
  12.5 0.7 copy-start.12
  17.9 56.3 %copy-start.1 = (bf16[13,256,512]{2,1,0:T(8,128)(2,1)}, bf16[13,256,512]{2,1,0:T(8,128)(2,1)S(1)}, u32[]{:S(2)}) copy-start(bf16[13,256,512]{2,1,0:T(8,128)(2,1)S(1)} %select_select_fusion.1) | copy-start | bytes 10223620
  18.0 367.4 %collective-permute-start.6 = (bf16[208,16,512]{2,1,0:T(8,128)(2,1)S(1)}, bf16[208,16,512]{2,1,0:T(8,128)(2,1)}, u32[]{:S(2)}, u32[]{:S(2)}) collective-permute-start(bf16[208,16,512]{2,1,0:T(8,128)(2,1)S(1)} %bitcast.278), channel_id=1, source_target_pairs={{0,16},{2,18},{4,20},{6,22},{8,24},{10,26},{12,28},{14,30},{1,17},... | collective-permute-start | bytes 10223624 | tf_op jit(solution)/shard_map/ppermute | solution.py:22
  20.0 6.7 %copy-start.29 = (f32[4608]{0:T(1024)S(1)}, f32[4608]{0:T(1024)}, u32[]{:S(2)}) copy-start(f32[4608]{0:T(1024)} %param.12) | copy-start | bytes 55300
  31.2 0.6 copy-start.6
  31.2 0.6 copy-start.8
  31.8 14.3 %copy-start.4 = (bf16[128,4,64]{0,2,1:T(8,128)(2,1)}, bf16[128,4,64]{0,2,1:T(8,128)(2,1)S(1)}, u32[]{:S(2)}) copy-start(bf16[128,4,64]{0,2,1:T(8,128)(2,1)S(1)} %get-tuple-element.43) | copy-start | bytes 196612
  31.8 14.3 %copy-start.5 = (bf16[128,4,64]{0,2,1:T(8,128)(2,1)}, bf16[128,4,64]{0,2,1:T(8,128)(2,1)S(1)}, u32[]{:S(2)}) copy-start(bf16[128,4,64]{0,2,1:T(8,128)(2,1)S(1)} %get-tuple-element.44) | copy-start | bytes 196612
  44.6 344.3 %collective-permute-start.2 = (bf16[208,16,512]{2,1,0:T(8,128)(2,1)}, bf16[208,16,512]{2,1,0:T(8,128)(2,1)}, u32[]{:S(2)}, u32[]{:S(2)}) collective-permute-start(bf16[208,16,512]{2,1,0:T(8,128)(2,1)} %bitcast.60.own), channel_id=1, source_target_pairs={{0,16},{2,18},{4,20},{6,22},{8,24},{10,26},{12,28},{14,30},{1,17},... | collective-permute-start | bytes 10223624 | tf_op jit(solution)/shard_map/ppermute | solution.py:22
  53.6 12.5 %copy-start.24 = (f32[16,8]{1,0:T(8,128)S(1)}, f32[16,8]{1,0:T(8,128)}, u32[]{:S(2)}) copy-start(f32[16,8]{1,0:T(8,128)} %copy-done.23) | copy-start | bytes 1540
  53.6 12.5 %copy-start.30 = (f32[4608]{0:T(1024)S(1)}, f32[4608]{0:T(1024)}, u32[]{:S(2)}) copy-start(f32[4608]{0:T(1024)} %param.12) | copy-start | bytes 55300
  66.0 5.8 %copy-start.7 = (f32[128,64]{0,1:T(8,128)S(1)}, f32[128,64]{0,1:T(8,128)}, u32[]{:S(2)}) copy-start(f32[128,64]{0,1:T(8,128)} %copy-done.6) | copy-start | bytes 98308
  66.1 5.8 %copy-start.9 = (f32[128,64]{0,1:T(8,128)S(1)}, f32[128,64]{0,1:T(8,128)}, u32[]{:S(2)}) copy-start(f32[128,64]{0,1:T(8,128)} %copy-done.8) | copy-start | bytes 98308
  66.1 7.4 %copy-start.20 = (s32[16,8]{1,0:T(8,128)S(1)}, s32[16,8]{1,0:T(8,128)}, u32[]{:S(2)}) copy-start(s32[16,8]{1,0:T(8,128)} %get-tuple-element.125) | copy-start | bytes 1540
  71.9 0.7 copy-start.3
  73.6 0.6 copy-start.11
  74.2 6.2 %copy-start.26 = (s32[16]{0:T(128)S(1)}, s32[16]{0:T(128)}, u32[]{:S(2)}) copy-start(s32[16]{0:T(128)} %copy-done.25) | copy-start | bytes 196
  97.5 22.0 %slice-start = ((pred[16,8,256]{2,1,0:T(8,128)(4,1)}), pred[2,8,256]{2,1,0:T(8,128)(4,1)S(1)}, s32[]{:S(2)}) async-start(pred[16,8,256]{2,1,0:T(8,128)(4,1)} %copy-done.11), calls=%async_computation | async-start | bytes 8192 | tf_op jit(solution)/shard_map/slice | solution.py:196
  104.0 6.9 %copy-start.27 = (pred[256]{0:T(512)(128)(4,1)S(1)}, pred[256]{0:T(512)(128)(4,1)}, u32[]{:S(2)}) copy-start(pred[256]{0:T(512)(128)(4,1)} %get-tuple-element.127) | copy-start | bytes 772
  110.8 12.0 %slice-start.1 = ((pred[16,8,256]{2,1,0:T(8,128)(4,1)}), pred[13,8,256]{2,1,0:T(8,128)(4,1)S(1)}, s32[]{:S(2)}) async-start(pred[16,8,256]{2,1,0:T(8,128)(4,1)} %copy-done.11), calls=%async_computation.1 | async-start | bytes 53248 | tf_op jit(solution)/shard_map/slice | solution.py:196
  126.4 4.2 %copy-start.22 = (pred[8,256]{1,0:T(8,128)(4,1)S(1)}, pred[8,256]{1,0:T(8,128)(4,1)}, u32[]{:S(2)}) copy-start(pred[8,256]{1,0:T(8,128)(4,1)} %slice_bitcast_fusion.6) | copy-start | bytes 6148
  133.0 6.5 %copy-start.10 = (bf16[16,4,128]{2,1,0:T(4,128)(2,1)S(1)}, bf16[16,4,128]{2,1,0:T(4,128)(2,1)}, u32[]{:S(2)}) copy-start(bf16[16,4,128]{2,1,0:T(4,128)(2,1)} %copy.128) | copy-start | bytes 49156
  133.0 6.6 %copy-start.13 = (bf16[1,2,8,512]{3,2,1,0:T(8,128)(2,1)S(1)}, bf16[1,2,8,512]{3,2,1,0:T(8,128)(2,1)}, u32[]{:S(2)}) copy-start(bf16[1,2,8,512]{3,2,1,0:T(8,128)(2,1)} %get-tuple-element.45) | copy-start | bytes 49156
  133.1 11.0 %copy-start.28 = (s32[16]{0:T(128)S(1)}, s32[16]{0:T(128)}, u32[]{:S(2)}) copy-start(s32[16]{0:T(128)} %get-tuple-element.105) | copy-start | bytes 196
  139.3 228.7 %collective-permute-start = (bf16[128,4608]{1,0:T(8,128)(2,1)}, bf16[128,4608]{1,0:T(8,128)(2,1)}, u32[]{:S(2)}, u32[]{:S(2)}) collective-permute-start(bf16[128,4608]{1,0:T(8,128)(2,1)} %convolution_convert_fusion), channel_id=1, source_target_pairs={{0,1},{1,0},{2,3},{3,2},{4,5},{5,4},{6,7},{7,6},{8,9},{9,8},{10,11... | collective-permute-start | bytes 3538952 | tf_op jit(solution)/shard_map/ppermute | solution.py:209
  139.6 210.8 %collective-permute-start.3 = (bf16[2,2,8,512]{3,2,1,0:T(8,128)(2,1)S(1)}, bf16[2,2,8,512]{3,2,1,0:T(8,128)(2,1)S(1)}, u32[]{:S(2)}, u32[]{:S(2)}) collective-permute-start(bf16[2,2,8,512]{3,2,1,0:T(8,128)(2,1)S(1)} %pad_maximum_fusion.2), channel_id=1, source_target_pairs={{0,16},{2,18},{4,20},{6,22},{8,24},{10,26},{12,28},{14,30},{1,17},... | collective-permute-start | bytes 98312 | tf_op jit(solution)/shard_map/ppermute | solution.py:22
  140.9 220.9 %collective-permute-start.7 = (bf16[32,16,512]{2,1,0:T(8,128)(2,1)}, bf16[32,16,512]{2,1,0:T(8,128)(2,1)}, u32[]{:S(2)}, u32[]{:S(2)}) collective-permute-start(bf16[32,16,512]{2,1,0:T(8,128)(2,1)} %slice.329), channel_id=1, source_target_pairs={{0,16},{2,18},{4,20},{6,22},{8,24},{10,26},{12,28},{14,30},{1,17},... | collective-permute-start | bytes 1572872 | tf_op jit(solution)/shard_map/ppermute | solution.py:22
  350.5 26.1 %collective-permute-start.4 = (bf16[32,16,512]{2,1,0:T(8,128)(2,1)}, bf16[32,16,512]{2,1,0:T(8,128)(2,1)}, u32[]{:S(2)}, u32[]{:S(2)}) collective-permute-start(bf16[32,16,512]{2,1,0:T(8,128)(2,1)} %slice.328), channel_id=1, source_target_pairs={{0,16},{2,18},{4,20},{6,22},{8,24},{10,26},{12,28},{14,30},{1,17},... | collective-permute-start | bytes 1572872 | tf_op jit(solution)/shard_map/ppermute | solution.py:22
  365.5 4.7 %copy-start.21 = (f32[4608]{0:T(1024)S(1)}, f32[4608]{0:T(1024)}, u32[]{:S(2)}) copy-start(f32[4608]{0:T(1024)} %param.13) | copy-start | bytes 55300
  374.0 18.4 %collective-permute-start.5 = (bf16[16,16,512]{2,1,0:T(8,128)(2,1)}, bf16[16,16,512]{2,1,0:T(8,128)(2,1)}, u32[]{:S(2)}, u32[]{:S(2)}) collective-permute-start(bf16[16,16,512]{2,1,0:T(8,128)(2,1)} %bitcast.74), channel_id=1, source_target_pairs={{0,16},{2,18},{4,20},{6,22},{8,24},{10,26},{12,28},{14,30},{1,17},... | collective-permute-start | bytes 786440 | tf_op jit(solution)/shard_map/ppermute | solution.py:22
  375.3 19.5 %collective-permute-start.1 = (bf16[16,16,512]{2,1,0:T(8,128)(2,1)}, bf16[16,16,512]{2,1,0:T(8,128)(2,1)}, u32[]{:S(2)}, u32[]{:S(2)}) collective-permute-start(bf16[16,16,512]{2,1,0:T(8,128)(2,1)} %bitcast.59), channel_id=1, source_target_pairs={{0,16},{2,18},{4,20},{6,22},{8,24},{10,26},{12,28},{14,30},{1,17},... | collective-permute-start | bytes 786440 | tf_op jit(solution)/shard_map/ppermute | solution.py:22
where the time goes:
time: 404 us; the launch traced here: 397 us
  waiting for transfers between devices  216 us (53%)
  local copies, waits for them, and re-layouts  70.9 us (18%)
  other arithmetic  48.9 us (12%)
  matrix products  33.7 us (8%)
  Pallas kernels  16.7 us (4%)
  starting transfers between devices  9.46 us (2%)
    ppermute x7, waiting for transfers between devices, shifted(): lax.ppermute(value, axis, [(source, source + steps) for source in range(i...  216 us
    select_n x8, other arithmetic, write_rows(): jnp.where((grid == step)[:, :, None], rows[:, step][:, None, :], cache)  27.6 us
    pallas_call x6, Pallas kernels, place(): pl.pallas_call(functools.partial(place_kernel, pages, group), out_shape=j...  16.7 us
    select_n x6, local copies, waits for them, and re-layouts, write_rows(): jnp.where((grid == step)[:, :, None], rows[:, step][:, None, :], cache)  16.7 us
    dot_general x1, local copies, waits for them, and re-layouts, shards(): queries = jnp.dot(normed, query_weight, preferred_element_type=jnp.float32)  12.5 us
    ppermute x7, starting transfers between devices, shifted(): lax.ppermute(value, axis, [(source, source + steps) for source in range(i...  9.2 us
  transfers between devices with their start and end apart: 8, of which 2 were waited for; matrix products, arithmetic and copies ran while one was open for 34% of the time, Pallas kernels for 4%

commit v1 on v0

--- a/solution.py
+++ b/solution.py
@@ -42,8 +42,11 @@
     return cache
 
 
-def place_kernel(pages, group, slots, flag, own, received, *rest):
-    out, held, in_sem, out_sem = rest[-4:]
+def place_kernel(pages, group, first_page, slots_in, own, received, *rest):
+    out, held, slots, slot_sem, in_sem, out_sem = rest[-6:]
+    is_target = lax.axis_index("replica") >= lax.axis_size("replica") // 2
+    slot_copy = pltpu.make_async_copy(slots_in, slots, slot_sem)
+    slot_copy.start()
     groups = [(low, min(group, pages - low)) for low in range(0, pages, group)]
 
     def load(source):
@@ -52,44 +55,46 @@
                 source.at[pl.ds(low, count)], held.at[pl.ds(low, count)], in_sem.at[index]
             ).start()
 
-    @pl.when(flag[0] != 0)
+    @pl.when(is_target)
     def _():
         load(received)
 
-    @pl.when(flag[0] == 0)
+    @pl.when(jnp.logical_not(is_target))
     def _():
         load(own)
 
+    slot_copy.wait()
     for index, (low, count) in enumerate(groups):
         pltpu.make_async_copy(
             own.at[pl.ds(low, count)], held.at[pl.ds(low, count)], in_sem.at[index]
         ).wait()
 
         def send(page, carry):
-            pltpu.make_async_copy(held.at[page], out.at[slots[page]], out_sem).start()
+            pltpu.make_async_copy(held.at[page], out.at[slots[first_page + page]], out_sem).start()
             return carry
 
         lax.fori_loop(low, low + count, send, 0, unroll=8)
     pltpu.make_async_copy(held, held, out_sem).wait()
 
 
-def place(region, slots, flag, own, received, total):
+def place(region, slots, first_page, own, received, total):
     pages = own.shape[0]
     group = 16
     anywhere = pl.BlockSpec(memory_space=pltpu.MemorySpace.HBM)
-    scalar = pl.BlockSpec(memory_space=pltpu.SMEM)
-    operands = (slots, flag, own, received) + (() if region is None else (region,))
+    operands = (slots, own, received) + (() if region is None else (region,))
     return pl.pallas_call(
-        functools.partial(place_kernel, pages, group),
+        functools.partial(place_kernel, pages, group, first_page),
         out_shape=jax.ShapeDtypeStruct((total,) + own.shape[1:], own.dtype),
-        in_specs=[scalar, scalar] + [anywhere] * (len(operands) - 2),
+        in_specs=[anywhere] * len(operands),
         out_specs=anywhere,
         scratch_shapes=[
             pltpu.VMEM(own.shape, own.dtype),
+            pltpu.SMEM(slots.shape, slots.dtype),
+            pltpu.SemaphoreType.DMA,
             pltpu.SemaphoreType.DMA((-(-pages // group),)),
             pltpu.SemaphoreType.DMA,
         ],
-        input_output_aliases={} if region is None else {4: 0},
+        input_output_aliases={} if region is None else {3: 0},
         cost_estimate=pl.CostEstimate(
             flops=0, bytes_accessed=2 * own.size * 2, transcendentals=0
         ),
@@ -125,7 +130,6 @@
     slot_ids = lax.dynamic_index_in_dim(slot_map, partner, 0, keepdims=False)
     is_target = replica >= half_count
     slots = jnp.where(is_target, slot_ids, jnp.arange(page_count, dtype=jnp.int32))
-    flag = is_target.astype(jnp.int32).reshape(1)
 
     def paged(rows):
         return rows.reshape(-1, page_len, kv_width)
@@ -135,14 +139,18 @@
 
     early = max(1, requests // 8)
     late = max(1, requests // 16)
-    cuts = ((0, early), (early, requests - late), (requests - late, requests))
+    cuts = {
+        "v": ((0, early), (early, requests - late), (requests - late, requests)),
+        "k": ((0, requests - late), (requests - late, requests)),
+    }
     caches = {
         "v": cache_values.reshape(requests, length, kv_width),
         "k": cache_keys.reshape(requests, length, kv_width),
     }
-    early_rows = {name: paged(caches[name][:early]) for name in caches}
+    early_rows = paged(caches["v"][:early])
+    early_rows = jnp.where(is_target, jnp.zeros_like(early_rows), early_rows)
     states, caches, early_rows = lax.optimization_barrier((states, caches, early_rows))
-    raw = {name: shift(early_rows[name]) for name in caches}
+    raw = shift(early_rows)
 
     rows_first = states.transpose(1, 0, 2)
     widened = rows_first.astype(jnp.float32)
@@ -170,12 +178,12 @@
     own = {
         name: [
             write_rows(caches[name][low:high], new[name][low:high], own_lengths[low:high])
-            for low, high in cuts
+            for low, high in cuts[name]
         ]
         for name in caches
     }
-    middle = {name: shift(paged(own[name][1])) for name in caches}
-    delta = shift(jnp.stack([new["k"][:early], new["v"][:early]]))
+    middle = {name: shift(paged(own[name][-2])) for name in caches}
+    delta = shift(new["v"][:early])
 
     queries = jnp.dot(normed, query_weight, preferred_element_type=jnp.float32)
     queries = (
@@ -185,21 +193,19 @@
     )
     grid = jnp.arange(length, dtype=jnp.int32)
     visible = grid[None, None, :] <= positions[:, :, None]
-    outs = []
-    for index, (low, high) in enumerate(cuts):
-        key_view = own["k"][index].reshape(high - low, length, kv_local, HD)
-        value_view = own["v"][index].reshape(high - low, length, kv_local, HD)
-        scores = jnp.einsum(
-            "rtkgd,rlkd->rktgl", queries[low:high], key_view, preferred_element_type=jnp.float32
-        )
-        scores = softcap * jnp.tanh(scores / (softcap * math.sqrt(query_scalar)))
-        expo = jnp.where(visible[low:high, None, :, None, :], jnp.exp(scores), 0.0)
-        weights = (expo / jnp.sum(expo, axis=-1, keepdims=True)).astype(jnp.bfloat16)
-        attended = jnp.einsum(
-            "rktgl,rlkd->rtkgd", weights, value_view, preferred_element_type=jnp.float32
-        )
-        outs.append(attended.astype(jnp.bfloat16).reshape((high - low) * steps, q_local * HD))
-    attended = jnp.concatenate(outs, axis=0)
+    whole = {name: jnp.concatenate(own[name], axis=0) for name in caches}
+    key_view = whole["k"].reshape(requests, length, kv_local, HD)
+    value_view = whole["v"].reshape(requests, length, kv_local, HD)
+    scores = jnp.einsum(
+        "rtkgd,rlkd->rktgl", queries, key_view, preferred_element_type=jnp.float32
+    )
+    scores = softcap * jnp.tanh(scores / (softcap * math.sqrt(query_scalar)))
+    expo = jnp.where(visible[:, None, :, None, :], jnp.exp(scores), 0.0)
+    weights = (expo / jnp.sum(expo, axis=-1, keepdims=True)).astype(jnp.bfloat16)
+    attended = jnp.einsum(
+        "rktgl,rlkd->rtkgd", weights, value_view, preferred_element_type=jnp.float32
+    )
+    attended = attended.astype(jnp.bfloat16).reshape(requests * steps, q_local * HD)
     partial_sum = jnp.dot(attended, out_weight, preferred_element_type=jnp.float32).astype(
         jnp.bfloat16
     )
@@ -211,26 +217,26 @@
     moved = (summed * inverse * post_gain).reshape(requests, steps, model_width)
     decoded = (widened + moved).astype(jnp.bfloat16).transpose(1, 0, 2)
 
-    last_k, last_v, decoded = lax.optimization_barrier((own["k"][2], own["v"][2], decoded))
+    last_k, last_v, decoded = lax.optimization_barrier((own["k"][-1], own["v"][-1], decoded))
     last = {"v": shift(paged(last_v)), "k": shift(paged(last_k))}
 
-    results = {}
-    for name, part in (("v", 1), ("k", 0)):
-        first = write_rows(
-            raw[name].reshape(early, length, kv_width), delta[part], pair_lengths[:early]
+    first = write_rows(raw.reshape(early, length, kv_width), delta, pair_lengths[:early])
+    received = {"v": (paged(first), middle["v"], last["v"]), "k": (middle["k"], last["k"])}
+
+    def fill(region, name, index, chunk):
+        low = cuts[name][index][0]
+        return place(
+            region, slots, low * per_request, paged(own[name][index]), chunk, page_count
         )
-        region = None
-        received = (paged(first), middle[name], last[name])
-        for index, (low, high) in enumerate(cuts):
-            region = place(
-                region,
-                slots[low * per_request : high * per_request],
-                flag,
-                paged(own[name][index]),
-                received[index],
-                page_count,
-            )
-        results[name] = region
+
+    placed_v = fill(None, "v", 0, received["v"][0])
+    placed_v = fill(placed_v, "v", 1, received["v"][1])
+    placed_v, middle_k = lax.optimization_barrier((placed_v, received["k"][0]))
+    placed_k = fill(None, "k", 0, middle_k)
+    placed_k, last_v = lax.optimization_barrier((placed_k, received["v"][2]))
+    placed_v = fill(placed_v, "v", 2, last_v)
+    placed_v, last_k = lax.optimization_barrier((placed_v, received["k"][1]))
+    results = {"v": placed_v, "k": fill(placed_k, "k", 1, last_k)}
     return (decoded, results["k"], results["v"])
 
 

time: 404 us -> 392 us (0.970)
  waiting for transfers between devices: 216 us -> 245 us
  local copies, waits for them, and re-layouts: 70.9 us -> 46.8 us
  Pallas kernels: 16.7 us -> 11.4 us
  matrix products: 33.7 us -> 28.9 us
    ppermute x7 -> x6, waiting for transfers between devices: 216 us -> 245 us  [shifted(): lax.ppermute(value, axis, [(source, source + steps) for source in range(i...]
    select_n x6 -> x0, local copies, waits for them, and re-layouts: 16.7 us -> none  [write_rows(): jnp.where((grid == step)[:, :, None], rows[:, step][:, None, :], cache)]
    concatenate x0 -> x2, local copies, waits for them, and re-layouts: none -> 12.8 us  [shards(): whole = {name: jnp.concatenate(own[name], axis=0) for name in caches}]
    slice x11 -> x0, local copies, waits for them, and re-layouts: 9.01 us -> none  [the longest x2 3.74 us: shards(): early_rows = {name: paged(caches[name][:early]) for name in caches}]
    concatenate x0 -> x2, other arithmetic: none -> 7.76 us  [shards(): whole = {name: jnp.concatenate(own[name], axis=0) for name in caches}]
    select_n x8 -> x6, other arithmetic: 27.6 us -> 21.2 us  [write_rows(): jnp.where((grid == step)[:, :, None], rows[:, step][:, None, :], cache)]
    concatenate x6 -> x2, other arithmetic: 5.68 us -> 0.11 us  [rotate(): jnp.concatenate([leading * cosine - trailing * sines, trailing * cosine +...]
    pallas_call x6 -> x5, Pallas kernels: 16.7 us -> 11.4 us  [place(): pl.pallas_call(functools.partial(place_kernel, pages, group, first_page),...]
  transfers between devices with their start and end apart: 8 -> 7, of which waited for: 2 -> 2; matrix products, arithmetic and copies ran while one was open for 34% -> 27% of each run, Pallas kernels for 4% -> 2%
where the time goes in v1:
time: 392 us; the launch traced here: 388 us
  waiting for transfers between devices  245 us (62%)
  local copies, waits for them, and re-layouts  46.8 us (12%)
  other arithmetic  46.7 us (12%)
  matrix products  28.9 us (7%)
  Pallas kernels  11.4 us (3%)
  starting transfers between devices  8.15 us (2%)
    ppermute x6, waiting for transfers between devices, shifted(): lax.ppermute(value, axis, [(source, source + steps) for source in range(i...  245 us
    select_n x6, other arithmetic, write_rows(): jnp.where((grid == step)[:, :, None], rows[:, step][:, None, :], cache)  21.2 us
    concatenate x2, local copies, waits for them, and re-layouts, shards(): whole = {name: jnp.concatenate(own[name], axis=0) for name in caches}  12.8 us
    dot_general x1, local copies, waits for them, and re-layouts, shards(): queries = jnp.dot(normed, query_weight, preferred_element_type=jnp.float32)  12.7 us
    pallas_call x5, Pallas kernels, place(): pl.pallas_call(functools.partial(place_kernel, pages, group, first_page),...  11.4 us
    ppermute x6, starting transfers between devices, shifted(): lax.ppermute(value, axis, [(source, source + steps) for source in range(i...  7.9 us
  transfers between devices with their start and end apart: 7, of which 2 were waited for; matrix products, arithmetic and copies ran while one was open for 27% of the time, Pallas kernels for 2%

profile of v1, /device:TPU:27, one launch (start us, length us, event | category | flops | bytes accessed | tf_op | source)
XLA Modules:
  0.0 388.2 jit_solution(3780343222572843662)
XLA Ops:
  0.7 1.9 slice_select_fusion
  2.5 2.6 fusion.1
  5.1 1.4 fusion.68
  6.7 4.0 %fusion.15 = bf16[128,512]{1,0:T(8,128)(2,1)S(1)} fusion(bf16[4608,512]{1,0:T(8,128)(2,1)} %param.16, f32[4608]{0:T(1024)} %param.12, f32[16,8]{1,0:T(8,128)S(1)} %add_rsqrt_fusion, bf16[8,16,4608]{2,1,0:T(8,128)(2,1)} %param.11), kind=kOutput, calls=%fused_computation.27 | convolution fusion | flops 606404608 | bytes 6048256 | tf_op jit(solution)/shard_map/dot_general | solution.py:168
  11.3 4.6 %select_select_fusion.1 = bf16[13,256,512]{2,1,0:T(8,128)(2,1)S(1)} fusion(bf16[16,256,512]{2,1,0:T(8,128)(2,1)S(1)} %bitcast.186, pred[13,256]{1,0:T(8,128)(4,1)S(1)} %get-tuple-element.118, pred[13,256]{1,0:T(8,128)(4,1)S(1)} %get-tuple-element.119, pred[13,256]{1,0:T(8,128)(4,1)S(1)} %get-tuple-element.120, pred[13,256]{1,0:T(8,128)(4,1)S(1)} %get-tuple-element.121, ...), kind=kLoop, calls=%fused_computation.4 | loop fusion | flops 13631488 | bytes 6948864 | tf_op jit(solution)/shard_map/jit(_where)/select_n | solution.py:41
  16.0 1.3 collective-permute-start.1
  18.1 6.8 %copy.113 = bf16[512,4608]{1,0:T(8,128)(2,1)} copy(bf16[512,4608]{0,1:T(8,128)(2,1)} %bitcast.187) | data formatting | bytes 9437184 | tf_op jit(solution)/shard_map/dot_general | solution.py:172
  24.8 4.2 %fusion.11 = f32[128,4,128]{0,2,1:T(8,128)S(1)} fusion(bf16[4,128,4608]{2,1,0:T(8,128)(2,1)} %bitcast.188, f32[4608]{0:T(1024)S(1)} %copy-done.28, f32[16,8]{1,0:T(8,128)S(1)} %add_rsqrt_fusion, bf16[8,16,4608]{2,1,0:T(8,128)(2,1)} %param.11), kind=kOutput, calls=%fused_computation.23 | convolution fusion | flops 606339072 | bytes 6179328 | tf_op jit(solution)/shard_map/dot_general | solution.py:172
  30.0 0.8 copy.105
  30.7 1.0 slice.276
  32.1 7.2 %select_select_fusion = bf16[15,256,512]{2,1,0:T(8,128)(2,1)} fusion(bf16[16,256,512]{2,1,0:T(8,128)(2,1)} %bitcast.190, pred[15,256]{1,0:T(8,128)(4,1)S(1)} %get-tuple-element.102, pred[15,256]{1,0:T(8,128)(4,1)S(1)} %get-tuple-element.103, pred[15,256]{1,0:T(8,128)(4,1)S(1)} %get-tuple-element.104, pred[15,256]{1,0:T(8,128)(4,1)S(1)} %get-tuple-element.105, ...), kind=kLoop, calls=%fused_computation.3 | loop fusion | flops 15728640 | bytes 8017920 | tf_op jit(solution)/shard_map/jit(_where)/select_n | solution.py:41
  39.3 1.5 collective-permute-start.4
  40.8 0.7 slice_bitcast_fusion.1
  44.9 0.7 slice_bitcast_fusion.2
  45.6 1.4 fusion.56
  47.6 0.7 slice_reduce_fusion.7
  48.4 2.0 select_select_fusion.5
  50.4 4.6 %pad_maximum_fusion.1 = bf16[16,256,512]{2,1,0:T(8,128)(2,1)} fusion(bf16[1,256,512]{2,1,0:T(8,128)(2,1)} %select_select_fusion.5, bf16[15,256,512]{2,1,0:T(8,128)(2,1)} %select_select_fusion), kind=kLoop, calls=%fused_computation.2 | loop fusion | flops 2097152 | bytes 8388608 | tf_op jit(solution)/shard_map/concatenate | solution.py:196
  54.9 6.4 %copy.106 = bf16[16,256,512]{1,2,0:T(8,128)(2,1)} copy(bf16[16,256,512]{2,1,0:T(8,128)(2,1)} %pad_maximum_fusion.1) | data formatting | bytes 8388608 | tf_op jit(solution)/shard_map/concatenate | solution.py:196
  61.4 12.7 %copy.116 = bf16[1024,4608]{1,0:T(8,128)(2,1)} copy(bf16[1024,4608]{0,1:T(8,128)(2,1)} %bitcast.182) | data formatting | bytes 18874368 | tf_op jit(solution)/shard_map/dot_general | solution.py:188
  74.1 5.7 %fusion.9 = f32[128,8,128]{0,2,1:T(8,128)S(1)} fusion(bf16[8,128,4608]{2,1,0:T(8,128)(2,1)} %bitcast.183, f32[4608]{0:T(1024)S(1)} %copy-done.29, f32[16,8]{1,0:T(8,128)S(1)} %copy-done.18, bf16[8,16,4608]{2,1,0:T(8,128)(2,1)} %param.11), kind=kOutput, calls=%fused_computation.21 | convolution fusion | flops 1210318848 | bytes 11160064 | tf_op jit(solution)/shard_map/dot_general | solution.py:188
  79.9 0.7 subtract_convert_fusion
  80.6 1.8 copy.101
  82.4 0.9 copy.102
  83.2 0.8 iota_compare_fusion
  84.1 2.0 select_select_fusion.4
  86.1 1.7 select_select_fusion.3
  87.9 0.8 copy-done.3
  88.7 3.2 pad_maximum_fusion
  91.9 6.4 %copy.99 = bf16[16,256,512]{1,2,0:T(8,128)(2,1)} copy(bf16[16,256,512]{2,1,0:T(8,128)(2,1)} %pad_maximum_fusion) | data formatting | bytes 8388608 | tf_op jit(solution)/shard_map/concatenate | solution.py:196
  98.3 4.1 %fusion.7 = f32[16,4,8,2,256]{4,2,3,1,0:T(8,128)} fusion(bf16[16,256,4,128,1]{1,3,4,2,0:T(8,128)(2,1)} %bitcast.180, pred[16,8,256]{2,1,0:T(8,128)(4,1)S(1)} %iota_compare_fusion, bf16[16,8,4,2,64]{4,1,0,3,2:T(8,128)(2,1)} %bitcast.194, bf16[16,8,4,2,64]{4,1,0,3,2:T(8,128)(2,1)} %bitcast.193), kind=kOutput, calls=%fused_computation.18 | convolution fusion | flops 68419584 | bytes 5537792 | tf_op jit(solution)/shard_map/rtkgd,rlkd->rktgl/dot_general | solution.py:199
  102.3 4.7 %convolution_convert_fusion.1 = bf16[16,4,128,8,2]{2,3,4,1,0:T(8,128)(2,1)} fusion(bf16[16,256,4,128,1]{1,3,4,2,0:T(8,128)(2,1)} %bitcast.192, f32[16,4,8,2,256]{4,2,3,1,0:T(8,128)} %fusion.7), kind=kOutput, calls=%fused_computation.19 | convolution fusion | flops 67765504 | bytes 5505024 | tf_op jit(solution)/shard_map/rktgl,rlkd->rtkgd/dot_general | solution.py:205
  107.1 6.2 %convolution_convert_fusion = bf16[128,4608]{1,0:T(8,128)(2,1)} fusion(bf16[128,1024]{1,0:T(8,128)(2,1)} %bitcast.195, bf16[1024,4608]{1,0:T(8,128)(2,1)} %param.17), kind=kOutput, calls=%fused_computation | convolution fusion | flops 1208549376 | bytes 10878976 | tf_op jit(solution)/shard_map/dot_general | solution.py:209
  113.6 1.3 collective-permute-start.2
  114.8 1.3 collective-permute-start.3
  117.0 242.0 %collective-permute-done.2 = bf16[2,8,512]{2,0,1:T(2,128)(2,1)S(1)} collective-permute-done((bf16[2,8,512]{2,0,1:T(2,128)(2,1)S(1)}, bf16[2,8,512]{2,0,1:T(2,128)(2,1)S(1)}, u32[]{:S(2)}, u32[]{:S(2)}) %collective-permute-start.2) | collective-permute-done | bytes 16416 | tf_op jit(solution)/shard_map/ppermute | solution.py:22
  359.0 2.1 multiply_reduce_fusion
  361.1 3.8 fusion.8
  365.0 1.3 collective-permute-start.5
  366.3 1.3 collective-permute-start.6
  367.6 2.8 collective-permute-done.3
  370.4 3.6 select_select_fusion.2.received
  374.0 1.8 shard_map.130.rest_0_
  375.8 2.6 copy.110
  378.4 2.9 shard_map.131.rest_0_
  381.3 3.4 shard_map.132.rest_0_
  384.7 1.7 shard_map.133
  386.4 1.7 shard_map.134
  (111 shorter events, 8.0 us)
Async XLA Ops:
  0.6 115.5 %copy-start = (s32[8,256]{1,0:T(8,128)S(1)}, s32[8,256]{1,0:T(8,128)}, u32[]{:S(2)}) copy-start(s32[8,256]{1,0:T(8,128)} %param.21) | copy-start | bytes 24580
  5.1 19.7 %copy-start.17 = (f32[16,8]{1,0:T(8,128)}, f32[16,8]{1,0:T(8,128)S(1)}, u32[]{:S(2)}) copy-start(f32[16,8]{1,0:T(8,128)S(1)} %add_rsqrt_fusion) | copy-start | bytes 1540
  6.5 35.1 %copy-start.16 = (s32[16]{0:T(128)}, s32[16]{0:T(128)S(1)}, u32[]{:S(2)}) copy-start(s32[16]{0:T(128)S(1)} %get-tuple-element.96) | copy-start | bytes 196
  6.7 4.7 %copy-start.2 = (bf16[256,16,512]{2,1,0:T(8,128)(2,1)S(1)}, bf16[256,16,512]{2,1,0:T(8,128)(2,1)}, u32[]{:S(2)}) copy-start(bf16[256,16,512]{2,1,0:T(8,128)(2,1)} %param.19) | copy-start | bytes 12582916
  10.7 0.7 copy-start.12
  16.0 71.9 %copy-start.1 = (bf16[13,256,512]{2,1,0:T(8,128)(2,1)}, bf16[13,256,512]{2,1,0:T(8,128)(2,1)S(1)}, u32[]{:S(2)}) copy-start(bf16[13,256,512]{2,1,0:T(8,128)(2,1)S(1)} %select_select_fusion.1) | copy-start | bytes 10223620
  16.0 362.4 %collective-permute-start.1 = (bf16[208,16,512]{2,1,0:T(8,128)(2,1)S(1)}, bf16[208,16,512]{2,1,0:T(8,128)(2,1)}, u32[]{:S(2)}, u32[]{:S(2)}) collective-permute-start(bf16[208,16,512]{2,1,0:T(8,128)(2,1)S(1)} %bitcast.178), channel_id=1, source_target_pairs={{0,16},{2,18},{4,20},{6,22},{8,24},{10,26},{12,28},{14,30},{1,17},... | collective-permute-start | bytes 10223624 | tf_op jit(solution)/shard_map/ppermute | solution.py:22
  18.0 6.8 %copy-start.28 = (f32[4608]{0:T(1024)S(1)}, f32[4608]{0:T(1024)}, u32[]{:S(2)}) copy-start(f32[4608]{0:T(1024)} %param.12) | copy-start | bytes 55300
  29.2 0.6 copy-start.8
  29.2 0.6 copy-start.10
  29.3 0.6 copy-start.4
  29.3 0.6 copy-start.6
  32.1 9.4 %copy-start.5 = (bf16[128,4,64]{0,2,1:T(8,128)(2,1)S(1)}, bf16[128,4,64]{0,2,1:T(8,128)(2,1)}, u32[]{:S(2)}) copy-start(bf16[128,4,64]{0,2,1:T(8,128)(2,1)} %copy-done.4) | copy-start | bytes 196612
  32.1 9.4 %copy-start.7 = (bf16[128,4,64]{0,2,1:T(8,128)(2,1)S(1)}, bf16[128,4,64]{0,2,1:T(8,128)(2,1)}, u32[]{:S(2)}) copy-start(bf16[128,4,64]{0,2,1:T(8,128)(2,1)} %copy-done.6) | copy-start | bytes 196612
  39.3 342.0 %collective-permute-start.4 = (bf16[240,16,512]{2,1,0:T(8,128)(2,1)}, bf16[240,16,512]{2,1,0:T(8,128)(2,1)}, u32[]{:S(2)}, u32[]{:S(2)}) collective-permute-start(bf16[240,16,512]{2,1,0:T(8,128)(2,1)} %bitcast.44.own), channel_id=1, source_target_pairs={{0,16},{2,18},{4,20},{6,22},{8,24},{10,26},{12,28},{14,30},{1,17},... | collective-permute-start | bytes 11796488 | tf_op jit(solution)/shard_map/ppermute | solution.py:22
  42.9 5.4 %copy-start.19 = (pred[256]{0:T(512)(128)(4,1)}, pred[256]{0:T(512)(128)(4,1)S(1)}, u32[]{:S(2)}) copy-start(pred[256]{0:T(512)(128)(4,1)S(1)} %get-tuple-element.125) | copy-start | bytes 772
  42.9 5.4 %copy-start.20 = (pred[256]{0:T(512)(128)(4,1)}, pred[256]{0:T(512)(128)(4,1)S(1)}, u32[]{:S(2)}) copy-start(pred[256]{0:T(512)(128)(4,1)S(1)} %get-tuple-element.126) | copy-start | bytes 772
  43.5 4.8 %copy-start.21 = (pred[256]{0:T(512)(128)(4,1)}, pred[256]{0:T(512)(128)(4,1)S(1)}, u32[]{:S(2)}) copy-start(pred[256]{0:T(512)(128)(4,1)S(1)} %get-tuple-element.127) | copy-start | bytes 772
  43.5 4.8 %copy-start.22 = (pred[256]{0:T(512)(128)(4,1)}, pred[256]{0:T(512)(128)(4,1)S(1)}, u32[]{:S(2)}) copy-start(pred[256]{0:T(512)(128)(4,1)S(1)} %get-tuple-element.128) | copy-start | bytes 772
  44.2 4.1 %copy-start.23 = (pred[256]{0:T(512)(128)(4,1)}, pred[256]{0:T(512)(128)(4,1)S(1)}, u32[]{:S(2)}) copy-start(pred[256]{0:T(512)(128)(4,1)S(1)} %get-tuple-element.129) | copy-start | bytes 772
  44.2 4.1 %copy-start.24 = (pred[256]{0:T(512)(128)(4,1)}, pred[256]{0:T(512)(128)(4,1)S(1)}, u32[]{:S(2)}) copy-start(pred[256]{0:T(512)(128)(4,1)S(1)} %get-tuple-element.130) | copy-start | bytes 772
  44.9 3.5 copy-start.25
  44.9 3.5 copy-start.26
  45.6 1.4 copy-start.13
  61.4 12.7 %copy-start.18 = (f32[16,8]{1,0:T(8,128)S(1)}, f32[16,8]{1,0:T(8,128)}, u32[]{:S(2)}) copy-start(f32[16,8]{1,0:T(8,128)} %copy-done.17) | copy-start | bytes 1540
  61.4 12.7 %copy-start.29 = (f32[4608]{0:T(1024)S(1)}, f32[4608]{0:T(1024)}, u32[]{:S(2)}) copy-start(f32[4608]{0:T(1024)} %param.12) | copy-start | bytes 55300
  74.1 5.8 %copy-start.9 = (f32[128,64]{0,1:T(8,128)S(1)}, f32[128,64]{0,1:T(8,128)}, u32[]{:S(2)}) copy-start(f32[128,64]{0,1:T(8,128)} %copy-done.8) | copy-start | bytes 98308
  74.1 5.8 %copy-start.11 = (f32[128,64]{0,1:T(8,128)S(1)}, f32[128,64]{0,1:T(8,128)}, u32[]{:S(2)}) copy-start(f32[128,64]{0,1:T(8,128)} %copy-done.10) | copy-start | bytes 98308
  87.9 0.8 copy-start.3
  107.1 6.5 %copy-start.14 = (bf16[2,8,512]{2,0,1:T(2,128)(2,1)S(1)}, bf16[2,8,512]{2,0,1:T(2,128)(2,1)}, u32[]{:S(2)}) copy-start(bf16[2,8,512]{2,0,1:T(2,128)(2,1)} %copy-done.13) | copy-start | bytes 49156
  107.1 9.7 %copy-start.27 = (s32[16]{0:T(128)S(1)}, s32[16]{0:T(128)}, u32[]{:S(2)}) copy-start(s32[16]{0:T(128)} %get-tuple-element.95) | copy-start | bytes 196
  107.1 254.1 %copy-start.15 = (f32[4608]{0:T(1024)S(1)}, f32[4608]{0:T(1024)}, u32[]{:S(2)}) copy-start(f32[4608]{0:T(1024)} %param.13) | copy-start | bytes 55300
  113.3 245.7 %collective-permute-start = (bf16[128,4608]{1,0:T(8,128)(2,1)}, bf16[128,4608]{1,0:T(8,128)(2,1)}, u32[]{:S(2)}, u32[]{:S(2)}) collective-permute-start(bf16[128,4608]{1,0:T(8,128)(2,1)} %convolution_convert_fusion), channel_id=1, source_target_pairs={{0,1},{1,0},{2,3},{3,2},{4,5},{5,4},{6,7},{7,6},{8,9},{9,8},{10,11... | collective-permute-start | bytes 3538952 | tf_op jit(solution)/shard_map/ppermute | solution.py:215
  113.6 245.4 %collective-permute-start.2 = (bf16[2,8,512]{2,0,1:T(2,128)(2,1)S(1)}, bf16[2,8,512]{2,0,1:T(2,128)(2,1)S(1)}, u32[]{:S(2)}, u32[]{:S(2)}) collective-permute-start(bf16[2,8,512]{2,0,1:T(2,128)(2,1)S(1)} %copy-done.14), channel_id=1, source_target_pairs={{0,16},{2,18},{4,20},{6,22},{8,24},{10,26},{12,28},{14,30},{1,17},... | collective-permute-start | bytes 49160 | tf_op jit(solution)/shard_map/ppermute | solution.py:22
  114.8 255.5 %collective-permute-start.3 = (bf16[32,16,512]{2,1,0:T(8,128)(2,1)}, bf16[32,16,512]{2,1,0:T(8,128)(2,1)}, u32[]{:S(2)}, u32[]{:S(2)}) collective-permute-start(bf16[32,16,512]{2,1,0:T(8,128)(2,1)} %slice_select_fusion), channel_id=1, source_target_pairs={{0,16},{2,18},{4,20},{6,22},{8,24},{10,26},{12,28},{14,30},{1,17},... | collective-permute-start | bytes 1572872 | tf_op jit(solution)/shard_map/ppermute | solution.py:22
  365.0 19.7 %collective-permute-start.5 = (bf16[16,16,512]{2,1,0:T(8,128)(2,1)}, bf16[16,16,512]{2,1,0:T(8,128)(2,1)}, u32[]{:S(2)}, u32[]{:S(2)}) collective-permute-start(bf16[16,16,512]{2,1,0:T(8,128)(2,1)} %bitcast.64), channel_id=1, source_target_pairs={{0,16},{2,18},{4,20},{6,22},{8,24},{10,26},{12,28},{14,30},{1,17},... | collective-permute-start | bytes 786440 | tf_op jit(solution)/shard_map/ppermute | solution.py:22
  366.3 20.1 %collective-permute-start.6 = (bf16[16,16,512]{2,1,0:T(8,128)(2,1)}, bf16[16,16,512]{2,1,0:T(8,128)(2,1)}, u32[]{:S(2)}, u32[]{:S(2)}) collective-permute-start(bf16[16,16,512]{2,1,0:T(8,128)(2,1)} %bitcast.65), channel_id=1, source_target_pairs={{0,16},{2,18},{4,20},{6,22},{8,24},{10,26},{12,28},{14,30},{1,17},... | collective-permute-start | bytes 786440 | tf_op jit(solution)/shard_map/ppermute | solution.py:22
